TPU v7x, 128 devices: a whole 4x4x4 slice. The times are simulated.
128 devices in a mesh: nodes: 16 (over x, z), cols: 8 (over y, core).
Axes of the slice: x: 4, y: 4, z: 4, core: 2. Of those that a mesh axis runs over, the one named last changes fastest.
Arguments:
- node_feats: bfloat16 [32768, 256], P(('nodes', 'cols')), may hold values from -6 to 6
- tile_row: int32 [16, 2816], P('nodes', 'cols'), may hold values from 0 to 15, as said below
- tile_col: int32 [16, 2816], P('nodes', 'cols'), may hold values from 0 to 31
- tile_bits: int32 [16, 2816, 16, 128], P('nodes', 'cols'), may hold values from 0 to 255, as said below
- w_self: bfloat16 [256, 256], replicated, may hold values from -0.375 to 0.375
- w_neigh: bfloat16 [256, 256], replicated, may hold values from -1.5 to 1.5
- bias: float32 [256], replicated, may hold values from -3 to 3
- cotangent: bfloat16 [32768, 256], P(('nodes', 'cols')), may hold values from -6 to 6
Outputs:
- layer_out: bfloat16 [32768, 256], P(('nodes', 'cols'))
- feat_grad: bfloat16 [32768, 256], P(('nodes', 'cols'))
- self_grad: float32 [256, 256], replicated
- neigh_grad: float32 [256, 256], replicated
- bias_grad: float32 [256], replicated
Inputs may be any that keep to these rules, and one draw needn't show every extreme that they name: `tile_row`: destination row block of a tile within its nodes group; in every nodes group at least one block carries no tile. `tile_col`: source row block of a tile within its cols index; a block may carry several tiles. `tile_bits`: bit j of word (w, a) of a tile is its edge from destination row a to source column 8 w + j; bits above the eighth are zero; some destination rows have no edge in any tile.
All inputs are finite; a program needn't handle non-finite values.
Results may differ from a plain program's by a relative error of at most 0.0075.
Values may be sent and summed in bfloat16 or wider, within the bound.
No kernel may reach another device: no remote copies, remote signals or barrier semaphores. Data moves between devices by JAX's collectives and lax.ppermute only.
A program may use at most 64 MiB of HBM per device.

v0:
```python
import math
import jax
import jax.numpy as jnp
from jax import lax
from jax.sharding import PartitionSpec as P


def unpack_tiles(packed):
    shifts = jnp.arange(8, dtype=jnp.int32)
    edge_flags = jnp.right_shift(packed[:, :, None, :], shifts[None, None, :, None]) & 1
    return edge_flags.reshape(packed.shape[0], 128, 128)


def shards(node_feats, tile_row, tile_col, tile_bits, w_self, w_neigh, bias, cotangent):
    rows_dev = node_feats.shape[0]
    width_in = node_feats.shape[1]
    node_count = lax.axis_size("nodes")
    col_count = lax.axis_size("cols")
    per_dev = rows_dev // 128
    dest_count = col_count * per_dev
    source_count = node_count * per_dev
    tile_count = tile_row.shape[1]
    tile_group = math.gcd(tile_count, 32)
    group_count = tile_count // tile_group
    rows_here = tile_row[0].reshape(group_count, tile_group)
    cols_here = tile_col[0].reshape(group_count, tile_group)
    packed_here = tile_bits[0].reshape(group_count, tile_group, 16, 128)
    source = lax.all_gather(node_feats, "nodes", axis=0, tiled=True)
    source_blocks = source.reshape(source_count, 128, width_in)

    def forward_step(totals, tile_set):
        summed, degree = totals
        rows_blk, cols_blk, packed_blk = tile_set
        edge_flags = unpack_tiles(packed_blk)
        bits_blk = edge_flags.astype(jnp.bfloat16)
        picked = source_blocks[cols_blk]
        products = jnp.einsum("tba,tbf->taf", bits_blk, picked, preferred_element_type=jnp.float32)
        summed = summed.at[rows_blk].add(products)
        degree = degree.at[rows_blk].add(jnp.sum(edge_flags, axis=1).astype(jnp.float32))
        return ((summed, degree), None)

    initial = (
        jnp.zeros((dest_count, 128, width_in), jnp.float32),
        jnp.zeros((dest_count, 128), jnp.float32),
    )
    (partial_sum, degree_part), _ = lax.scan(
        forward_step, initial, (rows_here, cols_here, packed_here)
    )
    summed, degree = (
        lax.psum_scatter(
            partial_sum.reshape(dest_count * 128, width_in), "cols", scatter_dimension=0, tiled=True
        ),
        lax.psum_scatter(
            degree_part.reshape(dest_count * 128), "cols", scatter_dimension=0, tiled=True
        ),
    )
    degree = jnp.maximum(degree, 1.0)
    neigh_mean = (summed / degree[:, None]).astype(jnp.bfloat16)
    preact = (
        jnp.dot(node_feats, w_self, preferred_element_type=jnp.float32)
        + jnp.dot(neigh_mean, w_neigh, preferred_element_type=jnp.float32)
        + bias
    )
    sigmoid_pre = jax.nn.sigmoid(preact)
    layer_out = (preact * sigmoid_pre).astype(jnp.bfloat16)
    pre_grad = (
        cotangent.astype(jnp.float32) * sigmoid_pre * (1.0 + preact * (1.0 - sigmoid_pre))
    ).astype(jnp.bfloat16)
    self_term = jnp.dot(node_feats.T, pre_grad, preferred_element_type=jnp.float32)
    neigh_term = jnp.dot(neigh_mean.T, pre_grad, preferred_element_type=jnp.float32)
    bias_term = jnp.sum(pre_grad.astype(jnp.float32), axis=0)
    self_grad, neigh_grad, bias_grad = lax.psum(
        (self_term, neigh_term, bias_term), ("nodes", "cols")
    )
    mean_grad = (
        jnp.dot(pre_grad, w_neigh.T, preferred_element_type=jnp.float32) / degree[:, None]
    ).astype(jnp.bfloat16)
    dest_grad = lax.all_gather(mean_grad, "cols", axis=0, tiled=True)
    grad_blocks = dest_grad.reshape(dest_count, 128, width_in)

    def backward_step(src_grad, tile_set):
        rows_blk, cols_blk, packed_blk = tile_set
        bits_blk = unpack_tiles(packed_blk).astype(jnp.bfloat16)
        picked = grad_blocks[rows_blk]
        products = jnp.einsum("tba,taf->tbf", bits_blk, picked, preferred_element_type=jnp.float32)
        return (src_grad.at[cols_blk].add(products), None)

    src_total, _ = lax.scan(
        backward_step,
        jnp.zeros((source_count, 128, width_in), jnp.float32),
        (rows_here, cols_here, packed_here),
    )
    src_total = src_total.reshape(source_count * 128, width_in)
    src_grad = lax.psum_scatter(src_total, "nodes", scatter_dimension=0, tiled=True)
    feat_grad = (jnp.dot(pre_grad, w_self.T, preferred_element_type=jnp.float32) + src_grad).astype(
        jnp.bfloat16
    )
    return (layer_out, feat_grad, self_grad, neigh_grad, bias_grad)


def solution(mesh):
    return jax.shard_map(
        shards,
        mesh=mesh,
        in_specs=(
            P(("nodes", "cols"), None),
            P("nodes", "cols"),
            P("nodes", "cols"),
            P("nodes", "cols", None, None),
            P(),
            P(),
            P(),
            P(("nodes", "cols"), None),
        ),
        out_specs=(P(("nodes", "cols"), None), P(("nodes", "cols"), None), P(), P(), P()),
        check_vma=False,
    )
```

profile of v0, /device:TPU:0, one launch (start us, length us, event | category | flops | bytes accessed | tf_op | source)
XLA Modules:
  0.0 557.2 jit_solution(13627646105467495376)
XLA Ops:
  9.5 48.4 %all-gather.3.cloned.1.call-done = bf16[4096,256]{1,0:T(8,128)(2,1)} async-done(((bf16[256,256]{1,0:T(8,128)(2,1)}), bf16[4096,256]{1,0:T(8,128)(2,1)}) %all-gather.3.cloned.1.call-update) | async-done | bytes 2097168 | tf_op jit(solution)/shard_map/all_gather | solution.py:28
  58.1 182.1 %while.22 = (s32[]{:T(128)}, f32[16,128,256]{2,1,0:T(8,128)S(1)}, f32[16,128]{1,0:T(8,128)S(1)}, s32[11,32]{1,0:T(8,128)S(1)}, s32[11,32,16,128]{3,2,1,0:T(8,128...) while((s32[]{:T(128)}, f32[16,128,256]{2,1,0:T(8,128)S(1)}, ...), condition=%wide.region_4.5_spmd, body=%wide.region_0.4_spmd.sunk | while | flops 272635072 | bytes 24165348 | solution.py:46
  67.2 6.5 %scatter_fusion = f32[16,128,256]{2,1,0:T(8,128)S(1)} fusion(f32[16,128,256]{2,1,0:T(8,128)S(1)} %get-tuple-element.232, s32[32]{0:T(128)S(1)} %get-tuple-element.213, f32[32,128,256]{2,1,0:T(8,128)} %fusion.56), kind=kCustom, calls=%fused_computation.2.clone.1 | custom fusion | flops 1048576 | bytes 12583040 | tf_op jit(solution)/shard_map/while/body/eval_jaxpr/scatter-add | solution.py:38
  83.8 6.5 %scatter_fusion = f32[16,128,256]{2,1,0:T(8,128)S(1)} fusion(f32[16,128,256]{2,1,0:T(8,128)S(1)} %get-tuple-element.232, s32[32]{0:T(128)S(1)} %get-tuple-element.213, f32[32,128,256]{2,1,0:T(8,128)} %fusion.56), kind=kCustom, calls=%fused_computation.2.clone.1 | custom fusion | flops 1048576 | bytes 12583040 | tf_op jit(solution)/shard_map/while/body/eval_jaxpr/scatter-add | solution.py:38
  116.9 6.5 %scatter_fusion = f32[16,128,256]{2,1,0:T(8,128)S(1)} fusion(f32[16,128,256]{2,1,0:T(8,128)S(1)} %get-tuple-element.232, s32[32]{0:T(128)S(1)} %get-tuple-element.213, f32[32,128,256]{2,1,0:T(8,128)} %fusion.56), kind=kCustom, calls=%fused_computation.2.clone.1 | custom fusion | flops 1048576 | bytes 12583040 | tf_op jit(solution)/shard_map/while/body/eval_jaxpr/scatter-add | solution.py:38
  133.5 6.5 %scatter_fusion = f32[16,128,256]{2,1,0:T(8,128)S(1)} fusion(f32[16,128,256]{2,1,0:T(8,128)S(1)} %get-tuple-element.232, s32[32]{0:T(128)S(1)} %get-tuple-element.213, f32[32,128,256]{2,1,0:T(8,128)} %fusion.56), kind=kCustom, calls=%fused_computation.2.clone.1 | custom fusion | flops 1048576 | bytes 12583040 | tf_op jit(solution)/shard_map/while/body/eval_jaxpr/scatter-add | solution.py:38
  216.2 6.5 %scatter_fusion = f32[16,128,256]{2,1,0:T(8,128)S(1)} fusion(f32[16,128,256]{2,1,0:T(8,128)S(1)} %get-tuple-element.232, s32[32]{0:T(128)S(1)} %get-tuple-element.213, f32[32,128,256]{2,1,0:T(8,128)} %fusion.56), kind=kCustom, calls=%fused_computation.2.clone.1 | custom fusion | flops 1048576 | bytes 12583040 | tf_op jit(solution)/shard_map/while/body/eval_jaxpr/scatter-add | solution.py:38
  243.1 13.7 %all-reduce = f32[2048]{0:T(1024)S(1)} all-reduce(f32[2048]{0:T(1024)S(1)} %bitcast.96), channel_id=3, replica_groups=mesh['nodes'=16,'cols'=8] {'cols'}, use_global_device_ids=true, to_apply=%region_6.7.clone | all-reduce | flops 2048 | bytes 16384
  256.9 17.8 %reduce-scatter.3.cloned.1.call-done = f32[256,256]{1,0:T(8,128)} async-done(((f32[2048,256]{1,0:T(8,128)}), f32[256,256]{1,0:T(8,128)}) %reduce-scatter.3.cloned.1.call-update) | async-done | bytes 262160 | tf_op jit(solution)/shard_map/reduce_scatter | solution.py:50
  280.3 20.2 %all-gather.5.cloned.1.call-done = bf16[2048,256]{1,0:T(8,128)(2,1)} async-done(((bf16[256,256]{1,0:T(8,128)(2,1)}), bf16[2048,256]{1,0:T(8,128)(2,1)}) %all-gather.5.cloned.1.call-update) | async-done | bytes 1048592 | tf_op jit(solution)/shard_map/all_gather | solution.py:78
  302.9 166.3 %while.23 = (s32[]{:T(128)}, f32[32,128,256]{2,1,0:T(8,128)}, s32[11,32]{1,0:T(8,128)}, s32[11,32,16,128]{3,2,1,0:T(8,128)}, s32[11,32]{1,0:T(8,128)}, /*index=5*/bf16[16,128,256]{2,1,0:T(8,128)(2,1)S(1)}, s32[]{:T(128)}) while((s32[]{:T(128)}, f32[32,128,256]{2,1,0:T(8,128)}, s32[11,32]{1,0:T(8,128)}, s32[11,32,16,128]{3,2,1,0:T(8,128)}, ...), condition=%wide.region_9.10_spmd, body=%wide.region_7.9_spmd.sunk | while | flops 271058112 | bytes 23862236 | solution.py:88
  308.1 9.9 %scatter_fusion.1 = f32[32,128,256]{2,1,0:T(8,128)} fusion(f32[32,128,256]{2,1,0:T(8,128)} %get-tuple-element.255, s32[32]{0:T(128)S(1)} %get-tuple-element.221, f32[32,128,256]{2,1,0:T(8,128)} %fusion.60), kind=kCustom, calls=%fused_computation.4.clone.1 | custom fusion | flops 1048576 | bytes 12583040 | tf_op jit(solution)/shard_map/while/body/eval_jaxpr/scatter-add | solution.py:86
  323.2 9.9 %scatter_fusion.1 = f32[32,128,256]{2,1,0:T(8,128)} fusion(f32[32,128,256]{2,1,0:T(8,128)} %get-tuple-element.255, s32[32]{0:T(128)S(1)} %get-tuple-element.221, f32[32,128,256]{2,1,0:T(8,128)} %fusion.60), kind=kCustom, calls=%fused_computation.4.clone.1 | custom fusion | flops 1048576 | bytes 12583040 | tf_op jit(solution)/shard_map/while/body/eval_jaxpr/scatter-add | solution.py:86
  338.3 9.9 %scatter_fusion.1 = f32[32,128,256]{2,1,0:T(8,128)} fusion(f32[32,128,256]{2,1,0:T(8,128)} %get-tuple-element.255, s32[32]{0:T(128)S(1)} %get-tuple-element.221, f32[32,128,256]{2,1,0:T(8,128)} %fusion.60), kind=kCustom, calls=%fused_computation.4.clone.1 | custom fusion | flops 1048576 | bytes 12583040 | tf_op jit(solution)/shard_map/while/body/eval_jaxpr/scatter-add | solution.py:86
  353.3 9.9 %scatter_fusion.1 = f32[32,128,256]{2,1,0:T(8,128)} fusion(f32[32,128,256]{2,1,0:T(8,128)} %get-tuple-element.255, s32[32]{0:T(128)S(1)} %get-tuple-element.221, f32[32,128,256]{2,1,0:T(8,128)} %fusion.60), kind=kCustom, calls=%fused_computation.4.clone.1 | custom fusion | flops 1048576 | bytes 12583040 | tf_op jit(solution)/shard_map/while/body/eval_jaxpr/scatter-add | solution.py:86
  368.4 9.9 %scatter_fusion.1 = f32[32,128,256]{2,1,0:T(8,128)} fusion(f32[32,128,256]{2,1,0:T(8,128)} %get-tuple-element.255, s32[32]{0:T(128)S(1)} %get-tuple-element.221, f32[32,128,256]{2,1,0:T(8,128)} %fusion.60), kind=kCustom, calls=%fused_computation.4.clone.1 | custom fusion | flops 1048576 | bytes 12583040 | tf_op jit(solution)/shard_map/while/body/eval_jaxpr/scatter-add | solution.py:86
  383.5 10.0 %scatter_fusion.1 = f32[32,128,256]{2,1,0:T(8,128)} fusion(f32[32,128,256]{2,1,0:T(8,128)} %get-tuple-element.255, s32[32]{0:T(128)S(1)} %get-tuple-element.221, f32[32,128,256]{2,1,0:T(8,128)} %fusion.60), kind=kCustom, calls=%fused_computation.4.clone.1 | custom fusion | flops 1048576 | bytes 12583040 | tf_op jit(solution)/shard_map/while/body/eval_jaxpr/scatter-add | solution.py:86
  398.7 10.2 %scatter_fusion.1 = f32[32,128,256]{2,1,0:T(8,128)} fusion(f32[32,128,256]{2,1,0:T(8,128)} %get-tuple-element.255, s32[32]{0:T(128)S(1)} %get-tuple-element.221, f32[32,128,256]{2,1,0:T(8,128)} %fusion.60), kind=kCustom, calls=%fused_computation.4.clone.1 | custom fusion | flops 1048576 | bytes 12583040 | tf_op jit(solution)/shard_map/while/body/eval_jaxpr/scatter-add | solution.py:86
  414.1 9.9 %scatter_fusion.1 = f32[32,128,256]{2,1,0:T(8,128)} fusion(f32[32,128,256]{2,1,0:T(8,128)} %get-tuple-element.255, s32[32]{0:T(128)S(1)} %get-tuple-element.221, f32[32,128,256]{2,1,0:T(8,128)} %fusion.60), kind=kCustom, calls=%fused_computation.4.clone.1 | custom fusion | flops 1048576 | bytes 12583040 | tf_op jit(solution)/shard_map/while/body/eval_jaxpr/scatter-add | solution.py:86
  429.1 10.0 %scatter_fusion.1 = f32[32,128,256]{2,1,0:T(8,128)} fusion(f32[32,128,256]{2,1,0:T(8,128)} %get-tuple-element.255, s32[32]{0:T(128)S(1)} %get-tuple-element.221, f32[32,128,256]{2,1,0:T(8,128)} %fusion.60), kind=kCustom, calls=%fused_computation.4.clone.1 | custom fusion | flops 1048576 | bytes 12583040 | tf_op jit(solution)/shard_map/while/body/eval_jaxpr/scatter-add | solution.py:86
  444.3 9.9 %scatter_fusion.1 = f32[32,128,256]{2,1,0:T(8,128)} fusion(f32[32,128,256]{2,1,0:T(8,128)} %get-tuple-element.255, s32[32]{0:T(128)S(1)} %get-tuple-element.221, f32[32,128,256]{2,1,0:T(8,128)} %fusion.60), kind=kCustom, calls=%fused_computation.4.clone.1 | custom fusion | flops 1048576 | bytes 12583040 | tf_op jit(solution)/shard_map/while/body/eval_jaxpr/scatter-add | solution.py:86
  459.4 9.8 %scatter_fusion.1 = f32[32,128,256]{2,1,0:T(8,128)} fusion(f32[32,128,256]{2,1,0:T(8,128)} %get-tuple-element.255, s32[32]{0:T(128)S(1)} %get-tuple-element.221, f32[32,128,256]{2,1,0:T(8,128)} %fusion.60), kind=kCustom, calls=%fused_computation.4.clone.1 | custom fusion | flops 1048576 | bytes 12583040 | tf_op jit(solution)/shard_map/while/body/eval_jaxpr/scatter-add | solution.py:86
  469.8 66.2 %psum.23 = f32[256]{0:T(256)} all-reduce(f32[256]{0:T(256)S(1)} %copy-done.7), channel_id=1, replica_groups=mesh['nodes'=16,'cols'=8] {'nodes','cols'}, use_global_device_ids=true, to_apply=%region_14.15 | all-reduce | flops 256 | bytes 2048 | tf_op jit(solution)/shard_map/psum | solution.py:72
  537.9 9.3 %reduce-scatter.5.cloned.1.call-done = f32[256,256]{1,0:T(8,128)} async-done(((f32[4096,256]{1,0:T(8,128)}), f32[256,256]{1,0:T(8,128)}) %reduce-scatter.5.cloned.1.call-update) | async-done | bytes 262160 | tf_op jit(solution)/shard_map/reduce_scatter | solution.py:94
  (234 shorter events, 224.6 us)
Async XLA Ops:
  7.2 267.5 %copy-start = (bf16[256,256]{1,0:T(8,128)(2,1)S(1)}, bf16[256,256]{1,0:T(8,128)(2,1)}, u32[]{:S(2)}) copy-start(bf16[256,256]{1,0:T(8,128)(2,1)} %param.17) | copy-start | bytes 393220
  7.2 50.7 %all-gather.3.cloned.1.call-start = ((), (), s32[]{:S(2)}) async-start(), calls=%async_computation.2 | async-start | bytes 2228224 | tf_op jit(solution)/shard_map/all_gather | solution.py:28
  7.9 266.8 %reduce-scatter.3.cloned.1.call-start = ((), (), s32[]{:S(2)}) async-start(), calls=%async_computation.3 | async-start | bytes 2359296 | tf_op jit(solution)/shard_map/reduce_scatter | solution.py:50
  240.2 1.4 copy-start.1
  240.2 2.0 copy-start.5
  240.2 2.0 copy-start.6
  240.3 1.4 copy-start.11
  240.3 2.6 copy-start.3
  240.3 2.6 copy-start.4
  240.3 34.4 %copy-start.9 = (bf16[256,256]{1,0:T(8,128)(2,1)S(1)}, bf16[256,256]{1,0:T(8,128)(2,1)}, u32[]{:S(2)}) copy-start(bf16[256,256]{1,0:T(8,128)(2,1)} %param.19) | copy-start | bytes 393220
  240.3 34.4 %copy-start.10 = (f32[256]{0:T(256)S(1)}, f32[256]{0:T(256)}, u32[]{:S(2)}) copy-start(f32[256]{0:T(256)} %param.18) | copy-start | bytes 3076
  241.6 58.9 %all-gather.5.cloned.1.call-start = ((), (), s32[]{:S(2)}) async-start(), calls=%async_computation.4 | async-start | bytes 1179648 | tf_op jit(solution)/shard_map/all_gather | solution.py:78
  274.7 4.5 copy-start.8
  278.2 257.9 %all-reduce.4.cloned.1.call-start = ((), (), s32[]{:S(2)}) async-start(), calls=%async_computation.6 | async-start | bytes 1048576 | tf_op jit(solution)/shard_map/psum | solution.py:72
  280.2 267.0 %reduce-scatter.5.cloned.1.call-start = ((), (), s32[]{:S(2)}) async-start(), calls=%async_computation.5 | async-start | bytes 4456448 | tf_op jit(solution)/shard_map/reduce_scatter | solution.py:94
  300.5 2.4 copy-start.2
  469.2 0.7 copy-start.7
Sparse Core Ops, SparseCore 0:
  10.2 47.7 all-gather.2
  241.7 32.9 reduce-scatter.2
  278.3 22.1 all-gather.4
  305.8 144.6 all-reduce.3
  469.3 77.8 reduce-scatter.4
where the time goes:
time: 560 us; the launch traced here: 557 us
  other arithmetic  200 us (36%)
  waiting for transfers between devices  96.4 us (17%)
  matrix products  85.6 us (15%)
  blocking collectives  80 us (14%)
  local copies, waits for them, and re-layouts  79.4 us (14%)
  between operations  14.6 us (3%)
    scatter-add x11, other arithmetic, backward_step(): return (src_grad.at[cols_blk].add(products), None)  109 us
    scatter-add x11, other arithmetic, forward_step(): summed = summed.at[rows_blk].add(products)  71.1 us
    psum x1, blocking collectives, shards(): lax.psum((self_term, neigh_term, bias_term), ('nodes', 'cols'))  66.2 us
    all_gather x1, waiting for transfers between devices, shards(): source = lax.all_gather(node_feats, 'nodes', axis=0, tiled=True)  48.4 us
    dot_general x11, matrix products, forward_step(): jnp.einsum('tba,tbf->taf', bits_blk, picked, preferred_element_type=jnp.f...  48.1 us
    gather x11, local copies, waits for them, and re-layouts, forward_step(): picked = source_blocks[cols_blk]  39.8 us
    dot_general x11, matrix products, backward_step(): jnp.einsum('tba,taf->tbf', bits_blk, picked, preferred_element_type=jnp.f...  30.1 us
    shift_right_arithmetic x66, local copies, waits for them, and re-layouts, unpack_tiles(): jnp.right_shift(packed[:, :, None, :], shifts[None, None, :, None]) & 1  23.4 us
  transfers between devices with their start and end apart: 5, of which 4 were waited for; matrix products, arithmetic and copies ran while one was open for 31% of the time, Pallas kernels for 0%

commit v1 on v0

--- a/solution.py
+++ b/solution.py
@@ -3,6 +3,28 @@
 import jax.numpy as jnp
 from jax import lax
 from jax.sharding import PartitionSpec as P
+
+
+def joined_along(blocks, dim):
+    blocks = jnp.moveaxis(blocks, 0, dim)
+    lengths = blocks.shape
+    return blocks.reshape(*lengths[:dim], lengths[dim] * lengths[dim + 1], *lengths[dim + 2 :])
+
+
+def ring_gather(x, axis, dim):
+    size = lax.axis_size(axis)
+    pairs = [(i, (i + 1) % size) for i in range(size)]
+    back = [(b, a) for a, b in pairs]
+    lower, upper = ([], [])
+    for step in range(size - 1):
+        if step % 2 == 0:
+            lower.append(lax.ppermute(lower[-1] if lower else x, axis, pairs))
+        else:
+            upper.append(lax.ppermute(upper[-1] if upper else x, axis, back))
+    blocks = jnp.stack([*lower[::-1], x, *upper])
+    shift = lax.axis_index(axis) - len(lower)
+    blocks = blocks[(jnp.arange(size) - shift) % size]
+    return joined_along(blocks, dim)
 
 
 def unpack_tiles(packed):
@@ -25,7 +47,7 @@
     rows_here = tile_row[0].reshape(group_count, tile_group)
     cols_here = tile_col[0].reshape(group_count, tile_group)
     packed_here = tile_bits[0].reshape(group_count, tile_group, 16, 128)
-    source = lax.all_gather(node_feats, "nodes", axis=0, tiled=True)
+    source = ring_gather(node_feats, "nodes", 0)
     source_blocks = source.reshape(source_count, 128, width_in)
 
     def forward_step(totals, tile_set):

time: 560 us -> 594 us (1.061)
  starting transfers between devices: 0.2 us -> 40.5 us
  waiting for transfers between devices: 96.4 us -> 75.2 us
  local copies, waits for them, and re-layouts: 79.4 us -> 88 us
  other arithmetic: 200 us -> 207 us
    all_gather x1 -> x0, waiting for transfers between devices: 48.4 us -> none  [shards(): source = lax.all_gather(node_feats, 'nodes', axis=0, tiled=True)]
    ppermute x0 -> x15, starting transfers between devices: none -> 40.2 us  [the longest x7 38.1 us: ring_gather(): upper.append(lax.ppermute(upper[-1] if upper else x, axis, back))]
    ppermute x0 -> x15, waiting for transfers between devices: none -> 26.2 us  [the longest x8 26.2 us: ring_gather(): lower.append(lax.ppermute(lower[-1] if lower else x, axis, pairs))]
    select_n x11, other arithmetic: 0.13 us -> 7.62 us  [forward_step(): summed = summed.at[rows_blk].add(products)]
  transfers between devices with their start and end apart: 5 -> 19, of which waited for: 4 -> 12; matrix products, arithmetic and copies ran while one was open for 31% -> 31% of each run, Pallas kernels for 0% -> 0%
where the time goes in v1:
time: 594 us; the launch traced here: 591 us
  other arithmetic  207 us (35%)
  local copies, waits for them, and re-layouts  88 us (15%)
  matrix products  85.9 us (14%)
  blocking collectives  78.4 us (13%)
  waiting for transfers between devices  75.2 us (13%)
  starting transfers between devices  40.5 us (7%)
  between operations  14.7 us (2%)
    scatter-add x11, other arithmetic, backward_step(): return (src_grad.at[cols_blk].add(products), None)  109 us
    scatter-add x11, other arithmetic, forward_step(): summed = summed.at[rows_blk].add(products)  71.1 us
    psum x1, blocking collectives, shards(): lax.psum((self_term, neigh_term, bias_term), ('nodes', 'cols'))  65.7 us
    dot_general x11, matrix products, forward_step(): jnp.einsum('tba,tbf->taf', bits_blk, picked, preferred_element_type=jnp.f...  48.4 us
    gather x11, local copies, waits for them, and re-layouts, forward_step(): picked = source_blocks[cols_blk]  39.8 us
    ppermute x7, starting transfers between devices, ring_gather(): upper.append(lax.ppermute(upper[-1] if upper else x, axis, back))  38.1 us
    dot_general x11, matrix products, backward_step(): jnp.einsum('tba,taf->tbf', bits_blk, picked, preferred_element_type=jnp.f...  30 us
    ppermute x8, waiting for transfers between devices, ring_gather(): lower.append(lax.ppermute(lower[-1] if lower else x, axis, pairs))  26.2 us
  transfers between devices with their start and end apart: 19, of which 12 were waited for; matrix products, arithmetic and copies ran while one was open for 31% of the time, Pallas kernels for 0%

profile of v1, /device:TPU:0, one launch (start us, length us, event | category | flops | bytes accessed | tf_op | source)
XLA Modules:
  0.0 590.8 jit_solution(16436282865309903777)
XLA Ops:
  9.3 8.0 %collective-permute-done = bf16[256,256]{1,0:T(8,128)(2,1)S(1)} collective-permute-done((bf16[256,256]{1,0:T(8,128)(2,1)}, bf16[256,256]{1,0:T(8,128)(2,1)S(1)}, u32[]{:S(2)}, u32[]{:S(2)}) %collective-permute-start) | collective-permute-done | bytes 131104 | tf_op jit(solution)/shard_map/ppermute | solution.py:21
  84.2 189.8 %while.22 = (s32[]{:T(128)}, f32[16,128,256]{2,1,0:T(8,128)S(1)}, f32[16,128]{1,0:T(8,128)S(1)}, s32[11,32]{1,0:T(8,128)}, s32[11,32,16,128]{3,2,1,0:T(8,128)}, ...) while((s32[]{:T(128)}, f32[16,128,256]{2,1,0:T(8,128)S(1)}, f32[16,128]{1,0:T(8,128)S(1)}, ...), condition=%wide.region_4.5_spmd, body=%wide.region_0.4_spmd.sunk | while | flops 272635072 | bytes 24165348 | solution.py:68
  94.0 6.5 %scatter_fusion = f32[16,128,256]{2,1,0:T(8,128)S(1)} fusion(f32[16,128,256]{2,1,0:T(8,128)S(1)} %get-tuple-element.232, s32[32]{0:T(128)S(1)} %get-tuple-element.213, f32[32,128,256]{2,1,0:T(8,128)} %fusion.58), kind=kCustom, calls=%fused_computation.3.clone.1 | custom fusion | flops 1048576 | bytes 12583040 | tf_op jit(solution)/shard_map/while/body/eval_jaxpr/scatter-add | solution.py:60
  111.2 6.5 %scatter_fusion = f32[16,128,256]{2,1,0:T(8,128)S(1)} fusion(f32[16,128,256]{2,1,0:T(8,128)S(1)} %get-tuple-element.232, s32[32]{0:T(128)S(1)} %get-tuple-element.213, f32[32,128,256]{2,1,0:T(8,128)} %fusion.58), kind=kCustom, calls=%fused_computation.3.clone.1 | custom fusion | flops 1048576 | bytes 12583040 | tf_op jit(solution)/shard_map/while/body/eval_jaxpr/scatter-add | solution.py:60
  145.7 6.5 %scatter_fusion = f32[16,128,256]{2,1,0:T(8,128)S(1)} fusion(f32[16,128,256]{2,1,0:T(8,128)S(1)} %get-tuple-element.232, s32[32]{0:T(128)S(1)} %get-tuple-element.213, f32[32,128,256]{2,1,0:T(8,128)} %fusion.58), kind=kCustom, calls=%fused_computation.3.clone.1 | custom fusion | flops 1048576 | bytes 12583040 | tf_op jit(solution)/shard_map/while/body/eval_jaxpr/scatter-add | solution.py:60
  163.0 6.5 %scatter_fusion = f32[16,128,256]{2,1,0:T(8,128)S(1)} fusion(f32[16,128,256]{2,1,0:T(8,128)S(1)} %get-tuple-element.232, s32[32]{0:T(128)S(1)} %get-tuple-element.213, f32[32,128,256]{2,1,0:T(8,128)} %fusion.58), kind=kCustom, calls=%fused_computation.3.clone.1 | custom fusion | flops 1048576 | bytes 12583040 | tf_op jit(solution)/shard_map/while/body/eval_jaxpr/scatter-add | solution.py:60
  249.2 6.5 %scatter_fusion = f32[16,128,256]{2,1,0:T(8,128)S(1)} fusion(f32[16,128,256]{2,1,0:T(8,128)S(1)} %get-tuple-element.232, s32[32]{0:T(128)S(1)} %get-tuple-element.213, f32[32,128,256]{2,1,0:T(8,128)} %fusion.58), kind=kCustom, calls=%fused_computation.3.clone.1 | custom fusion | flops 1048576 | bytes 12583040 | tf_op jit(solution)/shard_map/while/body/eval_jaxpr/scatter-add | solution.py:60
  276.8 12.7 %all-reduce = f32[2048]{0:T(1024)S(1)} all-reduce(f32[2048]{0:T(1024)S(1)} %bitcast.130), channel_id=3, replica_groups=mesh['nodes'=16,'cols'=8] {'cols'}, use_global_device_ids=true, to_apply=%region_6.7.clone | all-reduce | flops 2048 | bytes 16384
  289.6 18.8 %reduce-scatter.3.cloned.1.call-done = f32[256,256]{1,0:T(8,128)} async-done(((f32[2048,256]{1,0:T(8,128)}), f32[256,256]{1,0:T(8,128)}) %reduce-scatter.3.cloned.1.call-update) | async-done | bytes 262160 | tf_op jit(solution)/shard_map/reduce_scatter | solution.py:72
  314.1 20.1 %all-gather.2.cloned.1.call-done = bf16[2048,256]{1,0:T(8,128)(2,1)} async-done(((bf16[256,256]{1,0:T(8,128)(2,1)}), bf16[2048,256]{1,0:T(8,128)(2,1)}) %all-gather.2.cloned.1.call-update) | async-done | bytes 1048592 | tf_op jit(solution)/shard_map/all_gather | solution.py:100
  336.7 166.0 %while.23 = (s32[]{:T(128)}, f32[32,128,256]{2,1,0:T(8,128)}, s32[11,32]{1,0:T(8,128)}, s32[11,32,16,128]{3,2,1,0:T(8,128)}, s32[11,32]{1,0:T(8,128)}, /*index=5*/bf16[16,128,256]{2,1,0:T(8,128)(2,1)S(1)}, s32[]{:T(128)}) while((s32[]{:T(128)}, f32[32,128,256]{2,1,0:T(8,128)}, s32[11,32]{1,0:T(8,128)}, s32[11,32,16,128]{3,2,1,0:T(8,128)}, ...), condition=%wide.region_9.10_spmd, body=%wide.region_7.9_spmd.sunk | while | flops 271058112 | bytes 23862236 | solution.py:110
  341.9 9.9 %scatter_fusion.1 = f32[32,128,256]{2,1,0:T(8,128)} fusion(f32[32,128,256]{2,1,0:T(8,128)} %get-tuple-element.255, s32[32]{0:T(128)S(1)} %get-tuple-element.221, f32[32,128,256]{2,1,0:T(8,128)} %fusion.62), kind=kCustom, calls=%fused_computation.5.clone.1 | custom fusion | flops 1048576 | bytes 12583040 | tf_op jit(solution)/shard_map/while/body/eval_jaxpr/scatter-add | solution.py:108
  357.0 9.9 %scatter_fusion.1 = f32[32,128,256]{2,1,0:T(8,128)} fusion(f32[32,128,256]{2,1,0:T(8,128)} %get-tuple-element.255, s32[32]{0:T(128)S(1)} %get-tuple-element.221, f32[32,128,256]{2,1,0:T(8,128)} %fusion.62), kind=kCustom, calls=%fused_computation.5.clone.1 | custom fusion | flops 1048576 | bytes 12583040 | tf_op jit(solution)/shard_map/while/body/eval_jaxpr/scatter-add | solution.py:108
  372.1 9.8 %scatter_fusion.1 = f32[32,128,256]{2,1,0:T(8,128)} fusion(f32[32,128,256]{2,1,0:T(8,128)} %get-tuple-element.255, s32[32]{0:T(128)S(1)} %get-tuple-element.221, f32[32,128,256]{2,1,0:T(8,128)} %fusion.62), kind=kCustom, calls=%fused_computation.5.clone.1 | custom fusion | flops 1048576 | bytes 12583040 | tf_op jit(solution)/shard_map/while/body/eval_jaxpr/scatter-add | solution.py:108
  387.1 9.9 %scatter_fusion.1 = f32[32,128,256]{2,1,0:T(8,128)} fusion(f32[32,128,256]{2,1,0:T(8,128)} %get-tuple-element.255, s32[32]{0:T(128)S(1)} %get-tuple-element.221, f32[32,128,256]{2,1,0:T(8,128)} %fusion.62), kind=kCustom, calls=%fused_computation.5.clone.1 | custom fusion | flops 1048576 | bytes 12583040 | tf_op jit(solution)/shard_map/while/body/eval_jaxpr/scatter-add | solution.py:108
  402.2 9.9 %scatter_fusion.1 = f32[32,128,256]{2,1,0:T(8,128)} fusion(f32[32,128,256]{2,1,0:T(8,128)} %get-tuple-element.255, s32[32]{0:T(128)S(1)} %get-tuple-element.221, f32[32,128,256]{2,1,0:T(8,128)} %fusion.62), kind=kCustom, calls=%fused_computation.5.clone.1 | custom fusion | flops 1048576 | bytes 12583040 | tf_op jit(solution)/shard_map/while/body/eval_jaxpr/scatter-add | solution.py:108
  417.3 9.9 %scatter_fusion.1 = f32[32,128,256]{2,1,0:T(8,128)} fusion(f32[32,128,256]{2,1,0:T(8,128)} %get-tuple-element.255, s32[32]{0:T(128)S(1)} %get-tuple-element.221, f32[32,128,256]{2,1,0:T(8,128)} %fusion.62), kind=kCustom, calls=%fused_computation.5.clone.1 | custom fusion | flops 1048576 | bytes 12583040 | tf_op jit(solution)/shard_map/while/body/eval_jaxpr/scatter-add | solution.py:108
  432.4 10.1 %scatter_fusion.1 = f32[32,128,256]{2,1,0:T(8,128)} fusion(f32[32,128,256]{2,1,0:T(8,128)} %get-tuple-element.255, s32[32]{0:T(128)S(1)} %get-tuple-element.221, f32[32,128,256]{2,1,0:T(8,128)} %fusion.62), kind=kCustom, calls=%fused_computation.5.clone.1 | custom fusion | flops 1048576 | bytes 12583040 | tf_op jit(solution)/shard_map/while/body/eval_jaxpr/scatter-add | solution.py:108
  447.7 9.9 %scatter_fusion.1 = f32[32,128,256]{2,1,0:T(8,128)} fusion(f32[32,128,256]{2,1,0:T(8,128)} %get-tuple-element.255, s32[32]{0:T(128)S(1)} %get-tuple-element.221, f32[32,128,256]{2,1,0:T(8,128)} %fusion.62), kind=kCustom, calls=%fused_computation.5.clone.1 | custom fusion | flops 1048576 | bytes 12583040 | tf_op jit(solution)/shard_map/while/body/eval_jaxpr/scatter-add | solution.py:108
  462.8 9.9 %scatter_fusion.1 = f32[32,128,256]{2,1,0:T(8,128)} fusion(f32[32,128,256]{2,1,0:T(8,128)} %get-tuple-element.255, s32[32]{0:T(128)S(1)} %get-tuple-element.221, f32[32,128,256]{2,1,0:T(8,128)} %fusion.62), kind=kCustom, calls=%fused_computation.5.clone.1 | custom fusion | flops 1048576 | bytes 12583040 | tf_op jit(solution)/shard_map/while/body/eval_jaxpr/scatter-add | solution.py:108
  477.9 9.8 %scatter_fusion.1 = f32[32,128,256]{2,1,0:T(8,128)} fusion(f32[32,128,256]{2,1,0:T(8,128)} %get-tuple-element.255, s32[32]{0:T(128)S(1)} %get-tuple-element.221, f32[32,128,256]{2,1,0:T(8,128)} %fusion.62), kind=kCustom, calls=%fused_computation.5.clone.1 | custom fusion | flops 1048576 | bytes 12583040 | tf_op jit(solution)/shard_map/while/body/eval_jaxpr/scatter-add | solution.py:108
  492.9 9.7 %scatter_fusion.1 = f32[32,128,256]{2,1,0:T(8,128)} fusion(f32[32,128,256]{2,1,0:T(8,128)} %get-tuple-element.255, s32[32]{0:T(128)S(1)} %get-tuple-element.221, f32[32,128,256]{2,1,0:T(8,128)} %fusion.62), kind=kCustom, calls=%fused_computation.5.clone.1 | custom fusion | flops 1048576 | bytes 12583040 | tf_op jit(solution)/shard_map/while/body/eval_jaxpr/scatter-add | solution.py:108
  503.3 65.7 %psum.23 = f32[256]{0:T(256)} all-reduce(f32[256]{0:T(256)S(1)} %copy-done.8), channel_id=1, replica_groups=mesh['nodes'=16,'cols'=8] {'nodes','cols'}, use_global_device_ids=true, to_apply=%region_14.15 | all-reduce | flops 256 | bytes 2048 | tf_op jit(solution)/shard_map/psum | solution.py:94
  570.9 9.9 %reduce-scatter.5.cloned.1.call-done = f32[256,256]{1,0:T(8,128)} async-done(((f32[4096,256]{1,0:T(8,128)}), f32[256,256]{1,0:T(8,128)}) %reduce-scatter.5.cloned.1.call-update) | async-done | bytes 262160 | tf_op jit(solution)/shard_map/reduce_scatter | solution.py:116
  (282 shorter events, 298.8 us)
Async XLA Ops:
  7.2 301.2 %copy-start = (bf16[256,256]{1,0:T(8,128)(2,1)S(1)}, bf16[256,256]{1,0:T(8,128)(2,1)}, u32[]{:S(2)}) copy-start(bf16[256,256]{1,0:T(8,128)(2,1)} %param.17) | copy-start | bytes 393220
  7.2 73.7 %copy-start.3 = (bf16[256,256]{1,0:T(8,128)(2,1)S(1)}, bf16[256,256]{1,0:T(8,128)(2,1)}, u32[]{:S(2)}) copy-start(bf16[256,256]{1,0:T(8,128)(2,1)} %param.12) | copy-start | bytes 393220
  7.2 301.2 %reduce-scatter.3.cloned.1.call-start = ((), (), s32[]{:S(2)}) async-start(), calls=%async_computation.2 | async-start | bytes 2359296 | tf_op jit(solution)/shard_map/reduce_scatter | solution.py:72
  7.2 10.1 %collective-permute-start = (bf16[256,256]{1,0:T(8,128)(2,1)}, bf16[256,256]{1,0:T(8,128)(2,1)S(1)}, u32[]{:S(2)}, u32[]{:S(2)}) collective-permute-start(bf16[256,256]{1,0:T(8,128)(2,1)} %param.12), channel_id=1, source_target_pairs={{0,8},{8,16},{16,24},{24,32},{32,40},{40,48},{48,56},{56,64},{64,7... | collective-permute-start | bytes 393224 | tf_op jit(solution)/shard_map/ppermute | solution.py:21
  17.3 8.3 %collective-permute-start.1 = (bf16[256,256]{1,0:T(8,128)(2,1)S(1)}, bf16[256,256]{1,0:T(8,128)(2,1)S(1)}, u32[]{:S(2)}, u32[]{:S(2)}) collective-permute-start(bf16[256,256]{1,0:T(8,128)(2,1)S(1)} %collective-permute-done), channel_id=1, source_target_pairs={{0,8},{8,16},{16,24},{24,32},{32,40},{40,48},{48,56},{56,64},{64,7... | collective-permute-start | bytes 393224 | tf_op jit(solution)/shard_map/ppermute | solution.py:21
  17.3 8.3 %collective-permute-start.8 = (bf16[256,256]{1,0:T(8,128)(2,1)}, bf16[256,256]{1,0:T(8,128)(2,1)S(1)}, u32[]{:S(2)}, u32[]{:S(2)}) collective-permute-start(bf16[256,256]{1,0:T(8,128)(2,1)} %param.12), channel_id=1, source_target_pairs={{8,0},{16,8},{24,16},{32,24},{40,32},{48,40},{56,48},{64,56},{72,6... | collective-permute-start | bytes 393224 | tf_op jit(solution)/shard_map/ppermute | solution.py:23
  25.6 8.3 %collective-permute-start.2 = (bf16[256,256]{1,0:T(8,128)(2,1)S(1)}, bf16[256,256]{1,0:T(8,128)(2,1)S(1)}, u32[]{:S(2)}, u32[]{:S(2)}) collective-permute-start(bf16[256,256]{1,0:T(8,128)(2,1)S(1)} %collective-permute-done.1), channel_id=1, source_target_pairs={{0,8},{8,16},{16,24},{24,32},{32,40},{40,48},{48,56},{56,64},{64,7... | collective-permute-start | bytes 393224 | tf_op jit(solution)/shard_map/ppermute | solution.py:21
  25.6 8.3 %collective-permute-start.9 = (bf16[256,256]{1,0:T(8,128)(2,1)S(1)}, bf16[256,256]{1,0:T(8,128)(2,1)S(1)}, u32[]{:S(2)}, u32[]{:S(2)}) collective-permute-start(bf16[256,256]{1,0:T(8,128)(2,1)S(1)} %collective-permute-done.8), channel_id=1, source_target_pairs={{8,0},{16,8},{24,16},{32,24},{40,32},{48,40},{56,48},{64,56},{72,6... | collective-permute-start | bytes 393224 | tf_op jit(solution)/shard_map/ppermute | solution.py:23
  33.9 8.3 %collective-permute-start.3 = (bf16[256,256]{1,0:T(8,128)(2,1)S(1)}, bf16[256,256]{1,0:T(8,128)(2,1)S(1)}, u32[]{:S(2)}, u32[]{:S(2)}) collective-permute-start(bf16[256,256]{1,0:T(8,128)(2,1)S(1)} %collective-permute-done.2), channel_id=1, source_target_pairs={{0,8},{8,16},{16,24},{24,32},{32,40},{40,48},{48,56},{56,64},{64,7... | collective-permute-start | bytes 393224 | tf_op jit(solution)/shard_map/ppermute | solution.py:21
  33.9 8.3 %collective-permute-start.10 = (bf16[256,256]{1,0:T(8,128)(2,1)S(1)}, bf16[256,256]{1,0:T(8,128)(2,1)S(1)}, u32[]{:S(2)}, u32[]{:S(2)}) collective-permute-start(bf16[256,256]{1,0:T(8,128)(2,1)S(1)} %collective-permute-done.9), channel_id=1, source_target_pairs={{8,0},{16,8},{24,16},{32,24},{40,32},{48,40},{56,48},{64,56},{72,6... | collective-permute-start | bytes 393224 | tf_op jit(solution)/shard_map/ppermute | solution.py:23
  42.2 8.3 %collective-permute-start.4 = (bf16[256,256]{1,0:T(8,128)(2,1)S(1)}, bf16[256,256]{1,0:T(8,128)(2,1)S(1)}, u32[]{:S(2)}, u32[]{:S(2)}) collective-permute-start(bf16[256,256]{1,0:T(8,128)(2,1)S(1)} %collective-permute-done.3), channel_id=1, source_target_pairs={{0,8},{8,16},{16,24},{24,32},{32,40},{40,48},{48,56},{56,64},{64,7... | collective-permute-start | bytes 393224 | tf_op jit(solution)/shard_map/ppermute | solution.py:21
  42.2 8.3 %collective-permute-start.11 = (bf16[256,256]{1,0:T(8,128)(2,1)S(1)}, bf16[256,256]{1,0:T(8,128)(2,1)S(1)}, u32[]{:S(2)}, u32[]{:S(2)}) collective-permute-start(bf16[256,256]{1,0:T(8,128)(2,1)S(1)} %collective-permute-done.10), channel_id=1, source_target_pairs={{8,0},{16,8},{24,16},{32,24},{40,32},{48,40},{56,48},{64,56},{72,6... | collective-permute-start | bytes 393224 | tf_op jit(solution)/shard_map/ppermute | solution.py:23
  50.5 8.9 %collective-permute-start.5 = (bf16[256,256]{1,0:T(8,128)(2,1)S(1)}, bf16[256,256]{1,0:T(8,128)(2,1)S(1)}, u32[]{:S(2)}, u32[]{:S(2)}) collective-permute-start(bf16[256,256]{1,0:T(8,128)(2,1)S(1)} %collective-permute-done.4), channel_id=1, source_target_pairs={{0,8},{8,16},{16,24},{24,32},{32,40},{40,48},{48,56},{56,64},{64,7... | collective-permute-start | bytes 393224 | tf_op jit(solution)/shard_map/ppermute | solution.py:21
  51.1 8.3 %collective-permute-start.12 = (bf16[256,256]{1,0:T(8,128)(2,1)S(1)}, bf16[256,256]{1,0:T(8,128)(2,1)S(1)}, u32[]{:S(2)}, u32[]{:S(2)}) collective-permute-start(bf16[256,256]{1,0:T(8,128)(2,1)S(1)} %collective-permute-done.11), channel_id=1, source_target_pairs={{8,0},{16,8},{24,16},{32,24},{40,32},{48,40},{56,48},{64,56},{72,6... | collective-permute-start | bytes 393224 | tf_op jit(solution)/shard_map/ppermute | solution.py:23
  59.3 17.6 %copy-start.6 = (bf16[256,256]{1,0:T(8,128)(2,1)}, bf16[256,256]{1,0:T(8,128)(2,1)S(1)}, u32[]{:S(2)}) copy-start(bf16[256,256]{1,0:T(8,128)(2,1)S(1)} %collective-permute-done.5) | copy-start | bytes 393220
  59.3 9.4 %collective-permute-start.6 = (bf16[256,256]{1,0:T(8,128)(2,1)S(1)}, bf16[256,256]{1,0:T(8,128)(2,1)S(1)}, u32[]{:S(2)}, u32[]{:S(2)}) collective-permute-start(bf16[256,256]{1,0:T(8,128)(2,1)S(1)} %collective-permute-done.5), channel_id=1, source_target_pairs={{0,8},{8,16},{16,24},{24,32},{32,40},{40,48},{48,56},{56,64},{64,7... | collective-permute-start | bytes 393224 | tf_op jit(solution)/shard_map/ppermute | solution.py:21
  59.4 12.1 %collective-permute-start.13 = (bf16[256,256]{1,0:T(8,128)(2,1)S(1)}, bf16[256,256]{1,0:T(8,128)(2,1)}, u32[]{:S(2)}, u32[]{:S(2)}) collective-permute-start(bf16[256,256]{1,0:T(8,128)(2,1)S(1)} %collective-permute-done.12), channel_id=1, source_target_pairs={{8,0},{16,8},{24,16},{32,24},{40,32},{48,40},{56,48},{64,56},{72,6... | collective-permute-start | bytes 393224 | tf_op jit(solution)/shard_map/ppermute | solution.py:23
  68.7 8.4 %collective-permute-start.7 = (bf16[256,256]{1,0:T(8,128)(2,1)S(1)}, bf16[256,256]{1,0:T(8,128)(2,1)}, u32[]{:S(2)}, u32[]{:S(2)}) collective-permute-start(bf16[256,256]{1,0:T(8,128)(2,1)S(1)} %collective-permute-done.6), channel_id=1, source_target_pairs={{0,8},{8,16},{16,24},{24,32},{32,40},{40,48},{48,56},{56,64},{64,7... | collective-permute-start | bytes 393224 | tf_op jit(solution)/shard_map/ppermute | solution.py:21
  71.5 10.4 %collective-permute-start.14 = (bf16[256,256]{1,0:T(8,128)(2,1)}, bf16[256,256]{1,0:T(8,128)(2,1)S(1)}, u32[]{:S(2)}, u32[]{:S(2)}) collective-permute-start(bf16[256,256]{1,0:T(8,128)(2,1)} %collective-permute-done.13), channel_id=1, source_target_pairs={{8,0},{16,8},{24,16},{32,24},{40,32},{48,40},{56,48},{64,56},{72,6... | collective-permute-start | bytes 393224 | tf_op jit(solution)/shard_map/ppermute | solution.py:23
  274.0 34.4 %copy-start.10 = (bf16[256,256]{1,0:T(8,128)(2,1)S(1)}, bf16[256,256]{1,0:T(8,128)(2,1)}, u32[]{:S(2)}) copy-start(bf16[256,256]{1,0:T(8,128)(2,1)} %param.19) | copy-start | bytes 393220
  274.0 34.4 %copy-start.11 = (f32[256]{0:T(256)S(1)}, f32[256]{0:T(256)}, u32[]{:S(2)}) copy-start(f32[256]{0:T(256)} %param.18) | copy-start | bytes 3076
  275.3 59.0 %all-gather.2.cloned.1.call-start = ((), (), s32[]{:S(2)}) async-start(), calls=%async_computation.3 | async-start | bytes 1179648 | tf_op jit(solution)/shard_map/all_gather | solution.py:100
  311.8 257.2 %all-reduce.4.cloned.1.call-start = ((), (), s32[]{:S(2)}) async-start(), calls=%async_computation.5 | async-start | bytes 1048576 | tf_op jit(solution)/shard_map/psum | solution.py:94
  313.9 266.9 %reduce-scatter.5.cloned.1.call-start = ((), (), s32[]{:S(2)}) async-start(), calls=%async_computation.4 | async-start | bytes 4456448 | tf_op jit(solution)/shard_map/reduce_scatter | solution.py:116
  (8 other events, 21.8 us)
Sparse Core Ops, SparseCore 0:
  275.4 32.9 reduce-scatter.2
  312.0 22.2 all-gather.1
  339.8 144.6 all-reduce.3
  502.8 77.9 reduce-scatter.4
